TPU v7x, 32 devices: a whole 2x2x4 slice. The times are simulated.
32 devices in a mesh: mod: 8 (over z, y), mode: 4 (over x, core).
Axes of the slice: x: 2, y: 2, z: 4, core: 2. Of those that a mesh axis runs over, the one named last changes fastest.
Arguments:
- mod_points: int32 [8], P('mod'), may hold values from 0 to 47
- pupil_mask: int32 [256, 256], P('mode'), may hold values 0 or 1
- phase_offset: float32 [256, 256], P('mode'), may hold values from -6 to 6
- modes: bfloat16 [16, 256, 256], P('mode', 'mod'), may hold values from -6 to 6
- block_map: int32 [8], replicated, may hold values from 0 to 7, each once
Outputs:
- tangent: float32 [512, 16, 512], P('mod', 'mode')
Inputs may be any that keep to these rules, and one draw needn't show every extreme that they name: `mod_points`: indices of points on a circle of 48 equally spaced modulation points; repeats are allowed. `block_map`: each of the 8 detector row blocks appears exactly once.
All inputs are finite; a program needn't handle non-finite values. No bound on the sum of `pupil_mask` on one device may be relied on, other than what follows from the above.
Results may differ from a plain program's by a relative error of at most 0.015.
Values may be sent and summed in bfloat16 or wider, within the bound.
A program may use at most 64 MiB of HBM per device.

v0:
```python
import math

import jax
import jax.numpy as jnp
from jax import lax
from jax.sharding import PartitionSpec as P

NPTS = 48


radius_cells = 6.0


def dft_table(left, right, length):
    turns = left[:, None] * right[None, :] % length
    angle = turns.astype(jnp.float32) * (2.0 * math.pi / length)
    norm = 1.0 / math.sqrt(length)
    return (
        (jnp.cos(angle) * norm).astype(jnp.bfloat16),
        (-jnp.sin(angle) * norm).astype(jnp.bfloat16),
    )


def complex_product(form, left, right):
    real = jnp.einsum(form, left[0], right[0], preferred_element_type=jnp.float32) - jnp.einsum(
        form, left[1], right[1], preferred_element_type=jnp.float32
    )
    imag = jnp.einsum(form, left[0], right[1], preferred_element_type=jnp.float32) + jnp.einsum(
        form, left[1], right[0], preferred_element_type=jnp.float32
    )
    return (real, imag)


def pyramid_parts(length):
    centred = jnp.arange(length, dtype=jnp.int32) - length // 2
    quarter = (jnp.abs(centred)[:, None] + jnp.abs(centred)[None, :]) % 4
    cos_part = (quarter == 0).astype(jnp.float32) - (quarter == 2).astype(jnp.float32)
    sin_part = (quarter == 1).astype(jnp.float32) - (quarter == 3).astype(jnp.float32)
    return (cos_part, sin_part)


def pupil_field(point, phase, mask):
    pupil = phase.shape[0]
    length = 2 * pupil
    theta = point.astype(jnp.float32) * (2.0 * math.pi / NPTS)
    centred = (jnp.arange(pupil, dtype=jnp.int32) - pupil // 2).astype(jnp.float32)
    tilt = (
        2.0
        * math.pi
        * radius_cells
        / length
        * (jnp.cos(theta) * centred[:, None] + jnp.sin(theta) * centred[None, :])
    )
    total = phase + tilt
    return (
        (mask * jnp.cos(total)).astype(jnp.bfloat16),
        (mask * jnp.sin(total)).astype(jnp.bfloat16),
    )


def tangent_terms(fields_re, fields_im, second):
    d_re, d_im = complex_product("fuv,pv->ufp", (fields_re, fields_im), second)
    return 2.0 * (d_re[:, :1] * d_re[:, 1:] + d_im[:, :1] * d_im[:, 1:])


def local(mod_points, pupil_mask, phase_offset, modes, block_map):
    mod_count = lax.axis_size("mod")
    mode_dev = modes.shape[0]
    point_dev = mod_points.shape[0]
    stacked = jnp.stack([phase_offset, pupil_mask.astype(jnp.float32)])
    whole = lax.all_gather(stacked, "mode", axis=1, tiled=True)
    phase = whole[0]
    mask = whole[1]
    pupil = phase.shape[0]
    length = 2 * pupil
    centred_pad = jnp.arange(length, dtype=jnp.int32) - length // 2
    centred_pupil = jnp.arange(pupil, dtype=jnp.int32) - pupil // 2
    first = dft_table(centred_pad, centred_pupil, length)
    second = dft_table(centred_pad, centred_pad, length)
    cos_part, sin_part = pyramid_parts(length)
    factor = float(length * length) / float(pupil * pupil * point_dev * mod_count)
    field_re, field_im = pupil_field(mod_points[0], phase, mask)
    part_re = field_re.astype(jnp.float32)
    part_im = field_im.astype(jnp.float32)
    values = lax.all_gather(modes, "mod", axis=1, tiled=True).astype(jnp.float32)
    shifted = ((-values * part_im).astype(jnp.bfloat16), (values * part_re).astype(jnp.bfloat16))
    columns = (first[0], first[1])
    real, imag = complex_product("un,fnp->fup", columns, shifted)
    own_re, own_im = complex_product("un,np->up", first, (field_re, field_im))
    a_re = jnp.concatenate([own_re[None], real], axis=0).astype(jnp.bfloat16)
    a_im = jnp.concatenate([own_im[None], imag], axis=0).astype(jnp.bfloat16)
    f_re, f_im = complex_product("fup,vp->fuv", (a_re, a_im), first)
    g_re = (cos_part * f_re - sin_part * f_im).astype(jnp.bfloat16)
    g_im = (cos_part * f_im + sin_part * f_re).astype(jnp.bfloat16)
    b_re, b_im = complex_product("um,fmv->fuv", second, (g_re, g_im))
    b_re = b_re.astype(jnp.bfloat16)
    b_im = b_im.astype(jnp.bfloat16)
    fields = (b_re, b_im)
    block_count = block_map.shape[0]
    block_rows = length // block_count
    b_re, b_im = fields
    total = tangent_terms(b_re, b_im, second)
    ordered = total.reshape(block_count, block_rows, mode_dev, length)[block_map].reshape(
        length, mode_dev, length
    )
    summed = lax.psum_scatter(
        ordered.astype(jnp.bfloat16), "mod", scatter_dimension=0, tiled=True
    ).astype(jnp.float32)
    return summed * factor


def solution(mesh):
    placed = (P("mod"), P("mode", None), P("mode", None), P("mode", "mod", None), P())
    return jax.shard_map(
        local, mesh=mesh, in_specs=placed, out_specs=P("mod", "mode", None), check_vma=False
    )
```

profile of v0, /device:TPU:0, one launch (start us, length us, event | category | flops | bytes accessed | tf_op | source)
XLA Modules:
  0.0 262.7 jit_solution(8415529460458168751)
XLA Ops:
  6.5 0.0 all-reduce.3.cloned.1.call-start
  7.4 0.8 convert_bitcast_fusion
  8.2 0.8 pad_maximum_fusion.6
  9.1 8.6 %all_gather.6 = f32[2,256,256]{2,1,0:T(8,128)S(1)} all-gather(f32[2,64,256]{2,1,0:T(8,128)S(1)} %pad_maximum_fusion.6), channel_id=1, replica_groups=mesh['mod'=8,'mode'=4] {'mode'}, dimensions={1}, use_global_device_ids=true | all-gather | bytes 655360 | tf_op jit(solution)/shard_map/all_gather | solution.py:71
  17.7 1.1 fusion.57
  18.9 1.2 fusion.51
  20.1 0.0 copy-done
  20.1 31.9 %all_gather.7 = bf16[4,256,256]{2,1,0:T(8,128)(2,1)S(1)} all-gather(bf16[4,32,256]{2,1,0:T(8,128)(2,1)S(1)} %copy-done), channel_id=1, replica_groups=mesh['mod'=8,'mode'=4] {'mod'}, dimensions={1}, use_global_device_ids=true | all-gather | bytes 589824 | tf_op jit(solution)/shard_map/all_gather | solution.py:85
  52.0 2.4 fusion.40
  54.4 4.3 %fusion.36 = f32[4,256,512]{2,1,0:T(8,128)} fusion(bf16[4,256,256]{2,1,0:T(8,128)(2,1)S(1)} %all_gather.7, f32[256,256]{1,0:T(8,128)S(1)} %get-tuple-element.9, s32[256]{0:T(256)S(1)} %iota_add_fusion.1, s32[512]{0:T(512)S(1)} %iota_add_fusion), kind=kOutput, calls=%fused_computation.71 | convolution fusion | flops 271319040 | bytes 2886656 | tf_op jit(solution)/shard_map/un,fnp->fup/dot_general | solution.py:28
  58.7 2.8 %fusion.4 = bf16[4,512,256]{1,2,0:T(8,128)(2,1)S(1)} fusion(f32[4,256,512]{2,1,0:T(8,128)S(1)} %fusion.40, bf16[4,256,256]{2,1,0:T(8,128)(2,1)S(1)} %all_gather.7, f32[256,256]{1,0:T(8,128)S(1)} %get-tuple-element.9, s32[256]{0:T(256)S(1)} %iota_add_fusion.1, s32[512]{0:T(512)S(1)} %iota_add_fusion), kind=kOutput, calls=%fused_computation.27 | convolution fusion | flops 272498688 | bytes 3935232 | tf_op jit(solution)/shard_map/un,fnp->fup/dot_general | solution.py:25
  61.5 2.1 fusion.53
  63.6 2.1 fusion.52
  65.7 2.4 fusion.9
  68.1 0.1 copy.27
  68.2 4.8 %fusion.17 = f32[5,512,512]{2,1,0:T(8,128)} fusion(bf16[4,512,256]{1,2,0:T(8,128)(2,1)S(1)} %fusion.4, bf16[1,512,256]{1,2,0:T(8,128)(2,1)S(1)} %copy.27, s32[256]{0:T(256)S(1)} %iota_add_fusion.1, s32[512]{0:T(512)S(1)} %iota_add_fusion), kind=kOutput, calls=%fused_computation.55 | convolution fusion | flops 673972224 | bytes 6556672 | tf_op jit(solution)/shard_map/fup,vp->fuv/dot_general | solution.py:28
  73.0 4.7 %fusion.18 = f32[5,512,512]{2,1,0:T(8,128)} fusion(bf16[4,512,256]{1,2,0:T(8,128)(2,1)S(1)} %fusion.4, bf16[1,512,256]{1,2,0:T(8,128)(2,1)S(1)} %copy.27, s32[256]{0:T(256)S(1)} %iota_add_fusion.1, s32[512]{0:T(512)S(1)} %iota_add_fusion), kind=kOutput, calls=%fused_computation.56 | convolution fusion | flops 673841152 | bytes 6556672 | tf_op jit(solution)/shard_map/fup,vp->fuv/dot_general | solution.py:25
  77.8 0.0 copy-done.3
  77.8 3.0 %fusion.5 = bf16[4,512,256]{1,2,0:T(8,128)(2,1)S(1)} fusion(f32[4,256,512]{2,1,0:T(8,128)S(1)} %copy-done.3, bf16[4,256,256]{2,1,0:T(8,128)(2,1)S(1)} %all_gather.7, f32[256,256]{1,0:T(8,128)S(1)} %get-tuple-element.10, s32[256]{0:T(256)S(1)} %iota_add_fusion.1, s32[512]{0:T(512)S(1)} %iota_add_fusion), kind=kOutput, calls=%fused_computation.28 | convolution fusion | flops 272760832 | bytes 3935232 | tf_op jit(solution)/shard_map/un,fnp->fup/dot_general | solution.py:28
  80.8 2.4 fusion.8
  83.2 0.1 copy.31
  83.3 0.0 slice-start
  83.3 0.8 convert_subtract_fusion.1
  84.1 0.0 slice-start.1
  84.2 5.6 %convolution_add_fusion = f32[5,512,512]{2,1,0:T(8,128)S(1)} fusion(f32[5,512,512]{2,1,0:T(8,128)} %fusion.17, bf16[4,512,256]{1,2,0:T(8,128)(2,1)S(1)} %fusion.5, bf16[1,512,256]{1,2,0:T(8,128)(2,1)S(1)} %copy.31, s32[256]{0:T(256)S(1)} %iota_add_fusion.1, s32[512]{0:T(512)S(1)} %iota_add_fusion), kind=kOutput, calls=%fused_computation.13 | convolution fusion | flops 675151872 | bytes 11799552 | tf_op jit(solution)/shard_map/fup,vp->fuv/dot_general | solution.py:28
  89.7 0.0 slice-done
  89.7 0.0 slice-done.1
  89.8 4.9 %add_convert_fusion.1 = (bf16[5,512,512]{2,1,0:T(8,128)(2,1)S(1)}, bf16[5,512,512]{2,1,0:T(8,128)(2,1)S(1)}) fusion(f32[5,512,512]{2,1,0:T(8,128)S(1)} %convolution_add_fusion, f32[512,512]{1,0:T(8,128)S(1)} %get-tuple-element.12, f32[512,512]{1,0:T(8,128)S(1)} %get-tuple-element.11, f32[5,512,512]{2,1,0:T(8,128)S(1)} %bitcast.96, ...), kind=kOutput, calls=%fused_computation.5 | convolution fusion | flops 685768704 | bytes 19139584 | tf_op jit(solution)/shard_map/fup,vp->fuv/dot_general | solution.py:25
  94.6 5.3 %fusion.30 = f32[5,512,512]{2,1,0:T(8,128)S(1)} fusion(bf16[5,512,512]{2,1,0:T(8,128)(2,1)S(1)} %get-tuple-element.5, s32[512]{0:T(512)S(1)} %iota_add_fusion), kind=kOutput, calls=%fused_computation.68 | convolution fusion | flops 1346371584 | bytes 7866368 | tf_op jit(solution)/shard_map/um,fmv->fuv/dot_general | solution.py:28
  100.0 5.4 %fusion.34 = f32[5,512,512]{2,1,0:T(8,128)S(1)} fusion(bf16[5,512,512]{2,1,0:T(8,128)(2,1)S(1)} %get-tuple-element.6, s32[512]{0:T(512)S(1)} %iota_add_fusion), kind=kOutput, calls=%fused_computation.70 | convolution fusion | flops 1346371584 | bytes 7866368 | tf_op jit(solution)/shard_map/um,fmv->fuv/dot_general | solution.py:25
  105.3 8.0 %fusion.2 = bf16[5,512,512]{1,2,0:T(8,128)(2,1)S(1)} fusion(f32[5,512,512]{2,1,0:T(8,128)S(1)} %fusion.34, bf16[5,512,512]{2,1,0:T(8,128)(2,1)S(1)} %get-tuple-element.5, s32[512]{0:T(512)S(1)} %iota_add_fusion), kind=kOutput, calls=%fused_computation.11 | convolution fusion | flops 1349255168 | bytes 10487808 | tf_op jit(solution)/shard_map/um,fmv->fuv/dot_general | solution.py:25
  113.4 5.3 %fusion.32 = f32[512,5,512]{0,2,1:T(8,128)S(1)} fusion(bf16[5,512,512]{1,2,0:T(8,128)(2,1)S(1)} %fusion.2, s32[512]{0:T(512)S(1)} %iota_add_fusion), kind=kOutput, calls=%fused_computation.69 | convolution fusion | flops 1346371584 | bytes 7866368 | tf_op jit(solution)/shard_map/fuv,pv->ufp/dot_general | solution.py:25
  118.7 5.4 %fusion.24 = f32[512,5,512]{0,2,1:T(8,128)S(1)} fusion(bf16[5,512,512]{1,2,0:T(8,128)(2,1)S(1)} %fusion.2, s32[512]{0:T(512)S(1)} %iota_add_fusion), kind=kOutput, calls=%fused_computation.67 | convolution fusion | flops 1346633728 | bytes 7866368 | tf_op jit(solution)/shard_map/fuv,pv->ufp/dot_general | solution.py:28
  124.1 7.7 %fusion.3 = bf16[5,512,512]{1,2,0:T(8,128)(2,1)S(1)} fusion(f32[5,512,512]{2,1,0:T(8,128)S(1)} %fusion.30, bf16[5,512,512]{2,1,0:T(8,128)(2,1)S(1)} %get-tuple-element.6, s32[512]{0:T(512)S(1)} %iota_add_fusion), kind=kOutput, calls=%fused_computation.12 | convolution fusion | flops 1349255168 | bytes 10487808 | tf_op jit(solution)/shard_map/um,fmv->fuv/dot_general | solution.py:28
  131.9 5.4 %subtract_bitcast_fusion = f32[512,5,512]{2,0,1:T(8,128)S(1)} fusion(f32[512,5,512]{0,2,1:T(8,128)S(1)} %fusion.32, bf16[5,512,512]{1,2,0:T(8,128)(2,1)S(1)} %fusion.3, s32[512]{0:T(512)S(1)} %iota_add_fusion), kind=kOutput, calls=%fused_computation.2 | convolution fusion | flops 1347944448 | bytes 13109248 | tf_op jit(solution)/shard_map/fuv,pv->ufp/dot_general | solution.py:25
  137.2 0.1 slice_bitcast_fusion.1
  137.3 0.0 copy-start.1
  137.3 5.3 %add_bitcast_fusion = f32[512,5,512]{2,0,1:T(8,128)S(1)} fusion(f32[512,5,512]{0,2,1:T(8,128)S(1)} %fusion.24, bf16[5,512,512]{1,2,0:T(8,128)(2,1)S(1)} %fusion.3, s32[512]{0:T(512)S(1)} %iota_add_fusion), kind=kOutput, calls=%fused_computation.1 | convolution fusion | flops 1347682304 | bytes 13109248 | tf_op jit(solution)/shard_map/fuv,pv->ufp/dot_general | solution.py:28
  142.7 0.1 slice_bitcast_fusion
  142.7 0.0 copy-done.1
  142.8 3.0 %fusion.1 = bf16[512,4,512]{2,0,1:T(8,128)(2,1)} fusion(f32[512,5,512]{2,0,1:T(8,128)S(1)} %add_bitcast_fusion, f32[512,5,512]{2,0,1:T(8,128)S(1)} %subtract_bitcast_fusion, f32[512,512]{1,0:T(8,128)S(1)} %slice_bitcast_fusion, f32[512,512]{1,0:T(8,128)S(1)} %slice_bitcast_fusion.1), kind=kLoop, calls=%fused_computation.9 | loop fusion | flops 5242880 | bytes 12582912 | tf_op jit(solution)/shard_map/mul | solution.py:63
  145.7 2.3 gather_fusion
  148.0 0.0 copy-start.2
  148.0 2.9 %copy.43 = bf16[8,64,4,512]{3,2,1,0:T(4,128)(2,1)} copy(bf16[8,64,4,512]{3,1,2,0:T(8,128)(2,1)S(1)} %gather_fusion) | data formatting | bytes 4194304 | tf_op jit(solution)/shard_map/convert_element_type | solution.py:107
  151.0 0.0 all-reduce.3.cloned.1.call-update
  151.0 0.6 dynamic-slice
  152.2 101.5 %all-reduce.3.cloned.1.call-done = bf16[512,4,512]{2,1,0:T(4,128)(2,1)} async-done(((bf16[512,4,512]{2,1,0:T(4,128)(2,1)}), bf16[512,4,512]{2,1,0:T(4,128)(2,1)}) %all-reduce.3.cloned.1.call-update) | async-done | bytes 2097168
  253.8 1.9 convert_multiply_fusion.1
  (10 shorter events, 0.0 us)
Async XLA Ops:
  6.5 13.5 %copy-start = (bf16[4,32,256]{2,1,0:T(8,128)(2,1)S(1)}, bf16[4,32,256]{2,1,0:T(8,128)(2,1)}, u32[]{:S(2)}) copy-start(bf16[4,32,256]{2,1,0:T(8,128)(2,1)} %param.8) | copy-start | bytes 196612
  6.5 247.2 %all-reduce.3.cloned.1.call-start = ((), (), s32[]{:S(2)}) async-start(), calls=%async_computation | async-start | bytes 4194304
  73.0 4.8 %copy-start.3 = (f32[4,256,512]{2,1,0:T(8,128)S(1)}, f32[4,256,512]{2,1,0:T(8,128)}, u32[]{:S(2)}) copy-start(f32[4,256,512]{2,1,0:T(8,128)} %fusion.36) | copy-start | bytes 6291460
  83.3 6.4 %slice-start = ((s8[5242880]{0:T(1024)(128)(4,1)}), s8[4194304]{0:T(1024)(128)(4,1)S(1)}, s32[]{:S(2)}) async-start(s8[5242880]{0:T(1024)(128)(4,1)} %bitcast.95), calls=%async_computation.1 | async-start | bytes 8388608
  84.1 5.6 %slice-start.1 = ((s8[5242880]{0:T(1024)(128)(4,1)}), s8[1048576]{0:T(1024)(128)(4,1)S(1)}, s32[]{:S(2)}) async-start(s8[5242880]{0:T(1024)(128)(4,1)} %bitcast.95), calls=%async_computation.2 | async-start | bytes 2097152
  137.3 5.4 %copy-start.1 = (s32[8]{0:T(128)S(1)}, s32[8]{0:T(128)}, u32[]{:S(2)}) copy-start(s32[8]{0:T(128)} %param.9) | copy-start | bytes 100
  148.0 3.0 %copy-start.2 = (u32[32]{0:T(128)S(1)}, u32[32]{0:T(128)}, u32[]{:S(2)}) copy-start(u32[32]{0:T(128)} %constant.67) | copy-start | bytes 388
Sparse Core Ops, SparseCore 0:
  151.1 102.5 all-reduce.2
where the time goes:
time: 267 us; the launch traced here: 263 us
  waiting for transfers between devices  102 us (38%)
  matrix products  89.3 us (33%)
  blocking collectives  40.6 us (15%)
  between operations  15.4 us (6%)
  other arithmetic  9.67 us (4%)
  local copies, waits for them, and re-layouts  6.24 us (2%)
    unnamed x2, waiting for transfers between devices  102 us
    all_gather x1, blocking collectives, local(): lax.all_gather(modes, 'mod', axis=1, tiled=True).astype(jnp.float32)  31.9 us
    dot_general x5, matrix products, complex_product(): jnp.einsum(form, left[1], right[0], preferred_element_type=jnp.float32)  24 us
    dot_general x5, matrix products, complex_product(): jnp.einsum(form, left[1], right[1], preferred_element_type=jnp.float32)  23.4 us
    dot_general x5, matrix products, complex_product(): jnp.einsum(form, left[0], right[1], preferred_element_type=jnp.float32)  21.9 us
    dot_general x5, matrix products, complex_product(): jnp.einsum(form, left[0], right[0], preferred_element_type=jnp.float32)  20 us
    all_gather x1, blocking collectives, local(): whole = lax.all_gather(stacked, 'mode', axis=1, tiled=True)  8.65 us
  transfers between devices with their start and end apart: 1, of which 1 were waited for; matrix products, arithmetic and copies ran while one was open for 0% of the time, Pallas kernels for 0%

commit v1 on v0

v1 whole, which is shorter than its diff:
```python
import functools
import math

import jax
import jax.numpy as jnp
import numpy as np
from jax import lax
from jax.experimental import pallas as pl
from jax.experimental.pallas import tpu as pltpu
from jax.sharding import PartitionSpec as P

NPTS = 48


radius_cells = 6.0


def operator_tables(pupil):
    length = 2 * pupil
    centred_pad = np.arange(length) - length // 2
    centred_pupil = np.arange(pupil) - pupil // 2
    first = np.exp(-2j * np.pi * (np.outer(centred_pad, centred_pupil) % length) / length)
    second = np.exp(-2j * np.pi * (np.outer(centred_pad, centred_pad) % length) / length)
    phasor = np.exp(0.5j * np.pi * (np.abs(centred_pad) % 4))
    whole = second @ (phasor[:, None] * first) / length
    mirror = (-np.arange(pupil)) % pupil
    hilbert = 2.0 * whole.imag[:pupil][mirror].T
    flip = np.zeros((pupil, pupil))
    flip[mirror, np.arange(pupil)] = 1.0
    return (
        whole.real.astype(np.float32),
        whole.imag.astype(np.float32),
        hilbert.astype(jnp.bfloat16),
        flip.astype(jnp.bfloat16),
    )


def tangent_kernel(
    factor, block_ref, points_ref, rows_re_ref, rows_im_ref, field_ref, modes_ref, hilbert_ref,
    flip_ref, out_ref, left_ref, weight_ref, rot_ref, bent_ref, wide_ref, own_ref, acc_ref,
):
    mods, pupil = points_ref.shape
    rows = rows_re_ref.shape[0]
    mode_dev = modes_ref.shape[0]
    f32 = jnp.float32
    bf16 = jnp.bfloat16
    theta = points_ref[...].astype(f32) * (2.0 * math.pi / NPTS)
    centred = (lax.broadcasted_iota(jnp.int32, (mods, pupil), 1) - pupil // 2).astype(f32)
    scale = 2.0 * math.pi * radius_cells / (2 * pupil)
    row_angle = scale * jnp.cos(theta) * centred
    col_angle = scale * jnp.sin(theta) * centred
    row_cos, row_sin = jnp.cos(row_angle), jnp.sin(row_angle)
    rot_ref[0] = jnp.cos(col_angle)
    rot_ref[1] = jnp.sin(col_angle)
    rows_re = rows_re_ref[...]
    rows_im = rows_im_ref[...]
    for k in range(mods):
        cos, sin = row_cos[k : k + 1], row_sin[k : k + 1]
        re = (rows_re * cos - rows_im * sin).astype(bf16)
        im = (rows_re * sin + rows_im * cos).astype(bf16)
        base = 2 * rows * k
        left_ref[base : base + rows, :pupil] = re
        left_ref[base : base + rows, pupil:] = -im
        left_ref[base + rows : base + 2 * rows, :pupil] = im
        left_ref[base + rows : base + 2 * rows, pupil:] = re

    def detector(own, mode):
        wide_ref[...] = jnp.dot(left_ref[...], weight_ref[...], preferred_element_type=f32)
        for k in range(mods):
            base = 2 * rows * k
            cos, sin = rot_ref[0, k : k + 1], rot_ref[1, k : k + 1]
            re = wide_ref[base : base + rows]
            im = wide_ref[base + rows : base + 2 * rows]
            turned_re = re * cos - im * sin
            turned_im = re * sin + im * cos
            wide_ref[base : base + rows] = turned_re
            wide_ref[base + rows : base + 2 * rows] = turned_im
            bent_ref[base : base + rows] = turned_re.astype(bf16)
            bent_ref[base + rows : base + 2 * rows] = turned_im.astype(bf16)
        side = jnp.dot(bent_ref[...], hilbert_ref[...], preferred_element_type=f32)
        total_low = total_high = None
        for k in range(mods):
            base = 2 * rows * k
            re = wide_ref[base : base + rows]
            im = wide_ref[base + rows : base + 2 * rows]
            side_re = side[base : base + rows]
            side_im = side[base + rows : base + 2 * rows]
            low_re, low_im = re - side_im, im + side_re
            high_re, high_im = re + side_im, im - side_re
            if own:
                own_ref[k, 0] = low_re
                own_ref[k, 1] = low_im
                own_ref[k, 2] = high_re
                own_ref[k, 3] = high_im
            else:
                low = own_ref[k, 0] * low_re + own_ref[k, 1] * low_im
                high = own_ref[k, 2] * high_re + own_ref[k, 3] * high_im
                total_low = low if total_low is None else total_low + low
                total_high = high if total_high is None else total_high + high
        if not own:
            for half, total in enumerate((total_low, total_high)):
                total = total * factor
                coarse = total.astype(bf16)
                fine = (total - coarse.astype(f32)).astype(bf16)
                placed = jnp.dot(coarse, flip_ref[...], preferred_element_type=f32) + jnp.dot(
                    fine, flip_ref[...], preferred_element_type=f32
                )
                out_ref[:, mode, half * pupil : (half + 1) * pupil] = placed

    weight_ref[:pupil] = field_ref[0]
    weight_ref[pupil:] = field_ref[1]
    detector(True, 0)
    for mode in range(mode_dev):
        values = modes_ref[mode].astype(f32)
        weight_ref[:pupil] = (-values * field_ref[1].astype(f32)).astype(bf16)
        weight_ref[pupil:] = (values * field_ref[0].astype(f32)).astype(bf16)
        detector(False, mode)


def tangent_call(block, points, field, modes, factor, rows, mods):
    mode_dev, pupil, _ = modes.shape
    rows_re, rows_im, hilbert, flip = operator_tables(pupil)
    whole = lambda *shape: pl.BlockSpec(shape, lambda i, b: (0,) * len(shape))
    picked = pl.BlockSpec((rows, pupil), lambda i, b: (b[0], 0))
    spec = pltpu.PrefetchScalarGridSpec(
        num_scalar_prefetch=1,
        grid=(1,),
        in_specs=[
            whole(mods, pupil),
            picked,
            picked,
            whole(2, pupil, pupil),
            whole(mode_dev, pupil, pupil),
            whole(pupil, pupil),
            whole(pupil, pupil),
        ],
        out_specs=whole(rows, mode_dev, 2 * pupil),
        scratch_shapes=[
            pltpu.VMEM((2 * rows * mods, 2 * pupil), jnp.bfloat16),
            pltpu.VMEM((2 * pupil, pupil), jnp.bfloat16),
            pltpu.VMEM((2, mods, pupil), jnp.float32),
            pltpu.VMEM((2 * rows * mods, pupil), jnp.bfloat16),
            pltpu.VMEM((2 * rows * mods, pupil), jnp.float32),
            pltpu.VMEM((mods, 4, rows, pupil), jnp.float32),
            pltpu.VMEM((rows, pupil), jnp.float32),
        ],
    )
    return pl.pallas_call(
        functools.partial(tangent_kernel, factor),
        grid_spec=spec,
        out_shape=jax.ShapeDtypeStruct((rows, mode_dev, 2 * pupil), jnp.float32),
        compiler_params=pltpu.CompilerParams(vmem_limit_bytes=48 * 1024 * 1024),
    )(block, points, rows_re, rows_im, field, modes, hilbert, flip)


def local(mod_points, pupil_mask, phase_offset, modes, block_map):
    mod_count = lax.axis_size("mod")
    mods = mod_points.shape[0] * mod_count
    pupil = modes.shape[2]
    length = 2 * pupil
    rows = length // block_map.shape[0]
    mask = pupil_mask.astype(jnp.float32)
    own = jnp.stack([mask * jnp.cos(phase_offset), mask * jnp.sin(phase_offset)])
    field = lax.all_gather(own.astype(jnp.bfloat16), "mode", axis=1, tiled=True)
    values = lax.all_gather(modes, "mod", axis=1, tiled=True)
    points = lax.all_gather(mod_points, "mod", axis=0, tiled=True)
    points = jnp.broadcast_to(points[:, None], (mods, pupil))
    block = lax.dynamic_slice(block_map, (lax.axis_index("mod"),), (1,))
    factor = 2.0 * 0.25 * float(length * length) / float(pupil * pupil * mods)
    return tangent_call(block, points, field, values, factor, rows, mods)


def solution(mesh):
    placed = (P("mod"), P("mode", None), P("mode", None), P("mode", "mod", None), P())
    return jax.shard_map(
        local, mesh=mesh, in_specs=placed, out_specs=P("mod", "mode", None), check_vma=False
    )
```

time: 267 us -> 62.5 us (0.23); the launches traced: 263 us -> 62.3 us
  waiting for transfers between devices: 102 us -> 0 us
  matrix products: 89.3 us -> 0 us
  between operations: 15.4 us -> 0.72 us
  blocking collectives: 40.6 us -> 50.5 us
  other arithmetic: 9.67 us -> 1.16 us
  Pallas kernels: 0 us -> 6.33 us
  local copies, waits for them, and re-layouts: 6.24 us -> 3.57 us
    unnamed x2 -> x0, waiting for transfers between devices: 102 us -> none
    dot_general x20 -> x0, matrix products: 89.3 us -> none  [the longest x5 24 us: complex_product(): jnp.einsum(form, left[1], right[0], preferred_element_type=jnp.float32)]
    unnamed x0 -> x1, blocking collectives: none -> 13.1 us
    pallas_call x0 -> x1, Pallas kernels: none -> 6.33 us  [tangent_call(): pl.pallas_call(functools.partial(tangent_kernel, factor), grid_spec=spec,...]
    mul x4 -> x0, other arithmetic: 5.97 us -> none  [the longest x1 2.98 us: tangent_terms(): return 2.0 * (d_re[:, :1] * d_re[:, 1:] + d_im[:, :1] * d_im[:, 1:])]
    all_gather x2, blocking collectives: 40.6 us -> 37.4 us  [the longest x1 31.5 us: local(): values = lax.all_gather(modes, 'mod', axis=1, tiled=True)]
    convert_element_type x1 -> x0, local copies, waits for them, and re-layouts: 2.93 us -> none  [local(): ordered.astype(jnp.bfloat16)]
  transfers between devices with their start and end apart: 1 -> 0, of which waited for: 1 -> 0; matrix products, arithmetic and copies ran while one was open for 0% -> 0% of each run, Pallas kernels for 0% -> 0%
where the time goes in v1:
time: 62.5 us; the launch traced here: 62.3 us
  blocking collectives  50.5 us (81%)
  Pallas kernels  6.33 us (10%)
  local copies, waits for them, and re-layouts  3.57 us (6%)
  other arithmetic  1.16 us (2%)
  between operations  0.72 us (1%)
    all_gather x1, blocking collectives, local(): values = lax.all_gather(modes, 'mod', axis=1, tiled=True)  31.5 us
    unnamed x1, blocking collectives  13.1 us
    pallas_call x1, Pallas kernels, tangent_call(): pl.pallas_call(functools.partial(tangent_kernel, factor), grid_spec=spec,...  6.33 us
    all_gather x1, blocking collectives, local(): field = lax.all_gather(own.astype(jnp.bfloat16), 'mode', axis=1, tiled=True)  5.91 us
    unnamed x17, local copies, waits for them, and re-layouts  2.92 us

profile of v1, /device:TPU:0, one launch (start us, length us, event | category | flops | bytes accessed | tf_op | source)
XLA Modules:
  0.0 62.3 jit_solution(3139814332471586672)
XLA Ops:
  0.0 0.0 copy-start.6
  0.7 0.0 copy-done.6
  0.7 0.6 dynamic-slice
  1.3 0.0 copy-start.5
  1.3 0.7 %copy-done.5 = s32[8]{0:T(128)S(1)} copy-done((s32[8]{0:T(128)S(1)}, s32[8]{0:T(128)}, u32[]{:S(2)}) %copy-start.5) | copy-done | bytes 56
  1.9 0.6 dynamic_slice.3.block_ref
  2.5 0.8 %dynamic-update-slice = s32[8]{0:T(128)S(1)} dynamic-update-slice(s32[8]{0:T(128)S(1)} %broadcast.1, s32[1]{0:T(128)S(6)} %copy.11, u32[]{:T(128)} %bitcast) | dynamic-update-slice | bytes 12
  3.3 13.1 %all-reduce = s32[8]{0:T(128)S(1)} all-reduce(s32[8]{0:T(128)S(1)} %dynamic-update-slice), channel_id=1, replica_groups=mesh['mod'=8,'mode'=4] {'mod'}, use_global_device_ids=true, to_apply=%add | all-reduce | flops 8 | bytes 64
  16.3 0.1 broadcast_in_dim.2.points_ref
  16.4 0.0 copy-start.4
  16.4 0.0 copy-start.2
  16.4 1.2 %fusion = (bf16[1,64,256]{2,1,0:T(8,128)(2,1)S(1)}, bf16[1,64,256]{2,1,0:T(8,128)(2,1)S(1)}) fusion(f32[64,256]{1,0:T(8,128)} %param.11, s32[64,256]{1,0:T(8,128)} %param.10), kind=kLoop, calls=%fused_computation.3 | loop fusion | flops 81920 | bytes 196608 | tf_op jit(solution)/shard_map/stack | solution.py:163
  17.6 0.0 copy-start.1
  17.6 0.0 copy-start
  17.6 5.9 %all_gather.10.field_ref = bf16[2,256,256]{2,1,0:T(8,128)(2,1)S(1)} all-gather(bf16[2,64,256]{2,1,0:T(8,128)(2,1)S(1)} %pad_maximum_fusion), channel_id=1, replica_groups=mesh['mod'=8,'mode'=4] {'mode'}, dimensions={1}, use_global_device_ids=true | all-gather | bytes 327680 | tf_op jit(solution)/shard_map/all_gather | solution.py:164
  23.5 0.0 copy-done.4
  23.5 31.5 %all_gather.11.modes_ref = bf16[4,256,256]{2,1,0:T(8,128)(2,1)S(1)} all-gather(bf16[4,32,256]{2,1,0:T(8,128)(2,1)S(1)} %copy-done.4), channel_id=1, replica_groups=mesh['mod'=8,'mode'=4] {'mod'}, dimensions={1}, use_global_device_ids=true | all-gather | bytes 589824 | tf_op jit(solution)/shard_map/all_gather | solution.py:165
  55.0 0.0 copy-done.2
  55.0 0.0 copy-done.1
  55.1 0.0 copy-done
  55.1 0.0 copy-start.3
  55.1 0.9 %copy-done.3 = bf16[256,256]{1,0:T(8,128)(2,1)S(1)} copy-done((bf16[256,256]{1,0:T(8,128)(2,1)S(1)}, bf16[256,256]{1,0:T(8,128)(2,1)}, u32[]{:S(2)}) %copy-start.3) | copy-done | bytes 131096
  56.0 6.3 %shard_map.91 = f32[64,4,512]{2,1,0:T(4,128)} custom-call(s32[1]{0:T(128)} %dynamic_slice.3.block_ref, s32[8,256]{1,0:T(8,128)S(1)} %broadcast_in_dim.2.points_ref, f32[512,256]{1,0:T(8,128)S(1)} %copy-done.1, f32[512,256]{1,0:T(8,128)S(1)} %copy-done, bf16[2,256,256]{2,1,0:T(8,128)(2,1)S(1)} %all_gather.10.field_ref, ...), custom_call_target="tpu_custom_call" | custom-call | tf_op jit(solution)/shard_map/pallas_call | solution.py:148
  (2 shorter events, 0.0 us)
Async XLA Ops:
  0.0 0.7 %copy-start.6 = (u32[32]{0:T(128)S(1)}, u32[32]{0:T(128)}, u32[]{:S(2)}) copy-start(u32[32]{0:T(128)} %constant.25) | copy-start | bytes 388
  1.3 0.7 %copy-start.5 = (s32[8]{0:T(128)S(1)}, s32[8]{0:T(128)}, u32[]{:S(2)}) copy-start(s32[8]{0:T(128)} %param.13) | copy-start | bytes 100
  16.4 7.1 %copy-start.4 = (bf16[4,32,256]{2,1,0:T(8,128)(2,1)S(1)}, bf16[4,32,256]{2,1,0:T(8,128)(2,1)}, u32[]{:S(2)}) copy-start(bf16[4,32,256]{2,1,0:T(8,128)(2,1)} %param.12) | copy-start | bytes 196612
  16.4 38.6 %copy-start.2 = (bf16[256,256]{1,0:T(8,128)(2,1)S(1)}, bf16[256,256]{1,0:T(8,128)(2,1)}, u32[]{:S(2)}) copy-start(bf16[256,256]{1,0:T(8,128)(2,1)} %constant.21.clone.flip_ref) | copy-start | bytes 393220
  17.6 37.5 %copy-start.1 = (f32[512,256]{1,0:T(8,128)S(1)}, f32[512,256]{1,0:T(8,128)}, u32[]{:S(2)}) copy-start(f32[512,256]{1,0:T(8,128)} %constant.18.clone.rows_re_ref) | copy-start | bytes 1572868
  17.6 37.5 %copy-start = (f32[512,256]{1,0:T(8,128)S(1)}, f32[512,256]{1,0:T(8,128)}, u32[]{:S(2)}) copy-start(f32[512,256]{1,0:T(8,128)} %constant.19.clone.rows_im_ref) | copy-start | bytes 1572868
  55.1 0.9 %copy-start.3 = (bf16[256,256]{1,0:T(8,128)(2,1)S(1)}, bf16[256,256]{1,0:T(8,128)(2,1)}, u32[]{:S(2)}) copy-start(bf16[256,256]{1,0:T(8,128)(2,1)} %constant.20.clone.hilbert_ref) | copy-start | bytes 393220

commit v2 on v1

--- a/solution.py
+++ b/solution.py
@@ -28,23 +28,23 @@
     flip = np.zeros((pupil, pupil))
     flip[mirror, np.arange(pupil)] = 1.0
     return (
-        whole.real.astype(np.float32),
-        whole.imag.astype(np.float32),
+        whole.imag[:pupil].astype(np.float32),
         hilbert.astype(jnp.bfloat16),
         flip.astype(jnp.bfloat16),
     )
 
 
 def tangent_kernel(
-    factor, block_ref, points_ref, rows_re_ref, rows_im_ref, field_ref, modes_ref, hilbert_ref,
-    flip_ref, out_ref, left_ref, weight_ref, rot_ref, bent_ref, wide_ref, own_ref, acc_ref,
+    factor, blocks_ref, points_ref, rows_ref, field_ref, modes_ref, hilbert_ref, flip_ref, out_ref,
+    left_ref, weight_ref, rot_ref, bent_ref, wide_ref, own_ref,
 ):
-    mods, pupil = points_ref.shape
-    rows = rows_re_ref.shape[0]
+    mods = points_ref.shape[0]
+    pupil = rows_ref.shape[0]
+    rows = out_ref.shape[0]
     mode_dev = modes_ref.shape[0]
     f32 = jnp.float32
     bf16 = jnp.bfloat16
-    theta = points_ref[...].astype(f32) * (2.0 * math.pi / NPTS)
+    theta = points_ref[...][:, 0, :1].astype(f32) * (2.0 * math.pi / NPTS)
     centred = (lax.broadcasted_iota(jnp.int32, (mods, pupil), 1) - pupil // 2).astype(f32)
     scale = 2.0 * math.pi * radius_cells / (2 * pupil)
     row_angle = scale * jnp.cos(theta) * centred
@@ -52,8 +52,17 @@
     row_cos, row_sin = jnp.cos(row_angle), jnp.sin(row_angle)
     rot_ref[0] = jnp.cos(col_angle)
     rot_ref[1] = jnp.sin(col_angle)
-    rows_re = rows_re_ref[...]
-    rows_im = rows_im_ref[...]
+    start = blocks_ref[lax.axis_index("mod")] * rows
+    sign = jnp.where(start < pupil, 1.0, -1.0).astype(f32)
+    start = lax.rem(start, pupil)
+    rows_im = sign * rows_ref[pl.ds(pl.multiple_of(start, rows), rows), :]
+    facing = lax.rem(
+        start
+        + lax.broadcasted_iota(jnp.int32, (rows, pupil), 0)
+        + lax.broadcasted_iota(jnp.int32, (rows, pupil), 1),
+        pupil,
+    )
+    rows_re = jnp.where(facing == 0, 0.5, 0.0).astype(f32)
     for k in range(mods):
         cos, sin = row_cos[k : k + 1], row_sin[k : k + 1]
         re = (rows_re * cos - rows_im * sin).astype(bf16)
@@ -117,24 +126,159 @@
         detector(False, mode)
 
 
-def tangent_call(block, points, field, modes, factor, rows, mods):
+def gather_kernel(
+    count_y, point_ref, mask_ref, phase_ref, modes_ref, points_ref, field_ref, values_ref,
+    own_point, own_field, local_sem, point_send, point_recv, field_send, field_recv, z_send,
+    z_recv, y_send, y_recv,
+):
+    mod_count = lax.axis_size("mod")
+    mode_count = lax.axis_size("mode")
+    count_z = mod_count // count_y
+    me, mine = lax.axis_index("mod"), lax.axis_index("mode")
+    y, z = lax.rem(me, count_y), me // count_y
+    mode_dev, share, pupil = modes_ref.shape
+    stripe = mask_ref.shape[0]
+    mesh = pl.DeviceIdType.MESH
+    along_z = [lax.rem(z + d, count_z) * count_y + y for d in range(1, count_z)]
+    from_z = [lax.rem(z + count_z - d, count_z) * count_y + y for d in range(1, count_z)]
+    along_y = [z * count_y + lax.rem(y + d, count_y) for d in range(1, count_y)]
+    beside = [lax.rem(mine + d, mode_count) for d in range(1, mode_count)]
+
+    barrier = pltpu.get_barrier_semaphore()
+    for peer in along_z + along_y:
+        pl.semaphore_signal(barrier, inc=1, device_id=(peer, mine), device_id_type=mesh)
+    for peer in beside:
+        pl.semaphore_signal(barrier, inc=1, device_id=(me, peer), device_id_type=mesh)
+
+    own_point[...] = jnp.full(own_point.shape, point_ref[0], jnp.int32)
+    mask = mask_ref[...].astype(jnp.float32)
+    own_field[0] = (mask * jnp.cos(phase_ref[...])).astype(jnp.bfloat16)
+    own_field[1] = (mask * jnp.sin(phase_ref[...])).astype(jnp.bfloat16)
+    pl.semaphore_wait(barrier, len(along_z) + len(along_y) + len(beside))
+
+    def lines(i):
+        return pl.ds(pl.multiple_of(i * share, share), share)
+
+    def send(source, target, sent, landed, peer):
+        copy = pltpu.make_async_remote_copy(
+            src_ref=source, dst_ref=target, send_sem=sent, recv_sem=landed,
+            device_id=peer, device_id_type=mesh,
+        )
+        copy.start()
+        return copy
+
+    copies = []
+    for d, peer in enumerate(along_z):
+        copies.append(
+            send(own_point, points_ref.at[me], point_send.at[d], point_recv.at[d], (peer, mine))
+        )
+    for d, peer in enumerate(along_y):
+        copies.append(
+            send(
+                own_point, points_ref.at[me], point_send.at[count_z - 1 + d],
+                point_recv.at[count_z - 1 + d], (peer, mine),
+            )
+        )
+    held = pl.ds(pl.multiple_of(mine * stripe, stripe), stripe)
+    field_copies = [
+        send(own_field, field_ref.at[:, held], field_send.at[d], field_recv.at[d], (me, peer))
+        for d, peer in enumerate(beside)
+    ]
+    z_copies = []
+    y_copies = []
+    for j in range(mode_dev):
+        here = values_ref.at[j, lines(me)]
+        z_copies.append([
+            send(modes_ref.at[j], here, z_send.at[j, d], z_recv.at[j, d], (peer, mine))
+            for d, peer in enumerate(along_z)
+        ])
+        y_copies.append([
+            send(modes_ref.at[j], here, y_send.at[j, 0, d], y_recv.at[j, 0, d], (peer, mine))
+            for d, peer in enumerate(along_y)
+        ])
+    stay = [
+        pltpu.make_async_copy(own_point, points_ref.at[me], local_sem.at[0]),
+        pltpu.make_async_copy(own_field, field_ref.at[:, held], local_sem.at[1]),
+        pltpu.make_async_copy(modes_ref, values_ref.at[:, lines(me)], local_sem.at[2]),
+    ]
+    for copy in stay:
+        copy.start()
+
+    for d, source in enumerate(from_z):
+        copies[d].wait_recv()
+        for e, peer in enumerate(along_y):
+            at = count_z - 1 + (d + 1) * len(along_y) + e
+            copies.append(
+                send(
+                    points_ref.at[source], points_ref.at[source], point_send.at[at],
+                    point_recv.at[at], (peer, mine),
+                )
+            )
+    for j in range(mode_dev):
+        for d, source in enumerate(from_z):
+            z_copies[j][d].wait_recv()
+            piece = values_ref.at[j, lines(source)]
+            for e, peer in enumerate(along_y):
+                y_copies[j].append(
+                    send(piece, piece, y_send.at[j, d + 1, e], y_recv.at[j, d + 1, e], (peer, mine))
+                )
+    for copy in stay:
+        copy.wait()
+    for copy in copies[count_z - 1 :]:
+        copy.wait_recv()
+    for copy in field_copies:
+        copy.wait_recv()
+    for j in range(mode_dev):
+        for copy in y_copies[j]:
+            copy.wait_recv()
+    for copy in copies + field_copies + sum(z_copies, []) + sum(y_copies, []):
+        copy.wait_send()
+
+
+def gather_call(mod_points, pupil_mask, phase_offset, modes):
+    mod_count = lax.axis_size("mod")
+    mode_count = lax.axis_size("mode")
+    mode_dev, share, pupil = modes.shape
+    count_y = 2 if mod_count % 2 == 0 else 1
+    count_z = mod_count // count_y
+    vmem = pl.BlockSpec(memory_space=pltpu.VMEM)
+    dma = pltpu.SemaphoreType.DMA
+    few = max(count_y - 1, 1)
+    points = count_z - 1 + count_z * few
+    return pl.pallas_call(
+        functools.partial(gather_kernel, count_y),
+        in_specs=[pl.BlockSpec(memory_space=pltpu.SMEM), vmem, vmem, vmem],
+        out_specs=(vmem, vmem, vmem),
+        out_shape=(
+            jax.ShapeDtypeStruct((mod_count, 8, 128), jnp.int32),
+            jax.ShapeDtypeStruct((2, pupil, pupil), jnp.bfloat16),
+            jax.ShapeDtypeStruct((mode_dev, pupil, pupil), jnp.bfloat16),
+        ),
+        scratch_shapes=[
+            pltpu.VMEM((8, 128), jnp.int32),
+            pltpu.VMEM((2, pupil_mask.shape[0], pupil), jnp.bfloat16),
+            dma((3,)),
+            dma((points,)),
+            dma((points,)),
+            dma((mode_count - 1,)),
+            dma((mode_count - 1,)),
+            dma((mode_dev, count_z - 1)),
+            dma((mode_dev, count_z - 1)),
+            dma((mode_dev, count_z, few)),
+            dma((mode_dev, count_z, few)),
+        ],
+        compiler_params=pltpu.CompilerParams(collective_id=0, has_side_effects=True),
+    )(mod_points, pupil_mask, phase_offset, modes)
+
+
+def tangent_call(block_map, points, field, modes, factor, rows, mods):
     mode_dev, pupil, _ = modes.shape
-    rows_re, rows_im, hilbert, flip = operator_tables(pupil)
-    whole = lambda *shape: pl.BlockSpec(shape, lambda i, b: (0,) * len(shape))
-    picked = pl.BlockSpec((rows, pupil), lambda i, b: (b[0], 0))
-    spec = pltpu.PrefetchScalarGridSpec(
-        num_scalar_prefetch=1,
-        grid=(1,),
-        in_specs=[
-            whole(mods, pupil),
-            picked,
-            picked,
-            whole(2, pupil, pupil),
-            whole(mode_dev, pupil, pupil),
-            whole(pupil, pupil),
-            whole(pupil, pupil),
-        ],
-        out_specs=whole(rows, mode_dev, 2 * pupil),
+    below, hilbert, flip = operator_tables(pupil)
+    vmem = pl.BlockSpec(memory_space=pltpu.VMEM)
+    return pl.pallas_call(
+        functools.partial(tangent_kernel, factor),
+        in_specs=[pl.BlockSpec(memory_space=pltpu.SMEM)] + [vmem] * 6,
+        out_specs=vmem,
         scratch_shapes=[
             pltpu.VMEM((2 * rows * mods, 2 * pupil), jnp.bfloat16),
             pltpu.VMEM((2 * pupil, pupil), jnp.bfloat16),
@@ -142,15 +286,10 @@
             pltpu.VMEM((2 * rows * mods, pupil), jnp.bfloat16),
             pltpu.VMEM((2 * rows * mods, pupil), jnp.float32),
             pltpu.VMEM((mods, 4, rows, pupil), jnp.float32),
-            pltpu.VMEM((rows, pupil), jnp.float32),
         ],
-    )
-    return pl.pallas_call(
-        functools.partial(tangent_kernel, factor),
-        grid_spec=spec,
         out_shape=jax.ShapeDtypeStruct((rows, mode_dev, 2 * pupil), jnp.float32),
         compiler_params=pltpu.CompilerParams(vmem_limit_bytes=48 * 1024 * 1024),
-    )(block, points, rows_re, rows_im, field, modes, hilbert, flip)
+    )(block_map, points, below, field, modes, hilbert, flip)
 
 
 def local(mod_points, pupil_mask, phase_offset, modes, block_map):
@@ -159,15 +298,9 @@
     pupil = modes.shape[2]
     length = 2 * pupil
     rows = length // block_map.shape[0]
-    mask = pupil_mask.astype(jnp.float32)
-    own = jnp.stack([mask * jnp.cos(phase_offset), mask * jnp.sin(phase_offset)])
-    field = lax.all_gather(own.astype(jnp.bfloat16), "mode", axis=1, tiled=True)
-    values = lax.all_gather(modes, "mod", axis=1, tiled=True)
-    points = lax.all_gather(mod_points, "mod", axis=0, tiled=True)
-    points = jnp.broadcast_to(points[:, None], (mods, pupil))
-    block = lax.dynamic_slice(block_map, (lax.axis_index("mod"),), (1,))
+    points, field, values = gather_call(mod_points, pupil_mask, phase_offset, modes)
     factor = 2.0 * 0.25 * float(length * length) / float(pupil * pupil * mods)
-    return tangent_call(block, points, field, values, factor, rows, mods)
+    return tangent_call(block_map, points, field, values, factor, rows, mods)
 
 
 def solution(mesh):

time: 62.5 us -> 31.3 us (0.50)
  blocking collectives: 50.5 us -> 0 us
  Pallas kernels: 6.33 us -> 24.9 us
  local copies, waits for them, and re-layouts: 3.57 us -> 5.25 us
  other arithmetic: 1.16 us -> 0 us
    all_gather x2 -> x0, blocking collectives: 37.4 us -> none  [the longest x1 31.5 us: local(): values = lax.all_gather(modes, 'mod', axis=1, tiled=True)]
    pallas_call x1 -> x2, Pallas kernels: 6.33 us -> 24.9 us  [the longest x1 18.5 us: gather_call(): pl.pallas_call(functools.partial(gather_kernel, count_y), in_specs=[pl.Bl...]
    unnamed x1 -> x0, blocking collectives: 13.1 us -> none
    unnamed x17 -> x14, local copies, waits for them, and re-layouts: 2.92 us -> 5.25 us
    another operation x2 -> x0, other arithmetic: 1.16 us -> none  [local(): jnp.stack([mask * jnp.cos(phase_offset), mask * jnp.sin(phase_offset)])]
where the time goes in v2:
time: 31.3 us; the launch traced here: 30.9 us
  Pallas kernels  24.9 us (80%)
  local copies, waits for them, and re-layouts  5.25 us (17%)
  between operations  0.72 us (2%)
    pallas_call x1, Pallas kernels, gather_call(): pl.pallas_call(functools.partial(gather_kernel, count_y), in_specs=[pl.Bl...  18.5 us
    pallas_call x1, Pallas kernels, tangent_call(): pl.pallas_call(functools.partial(tangent_kernel, factor), in_specs=[pl.Bl...  6.48 us
    unnamed x14, local copies, waits for them, and re-layouts  5.25 us

profile of v2, /device:TPU:0, one launch (start us, length us, event | category | flops | bytes accessed | tf_op | source)
XLA Modules:
  0.0 30.9 jit_solution(6035029675459729831)
XLA Ops:
  0.0 0.0 copy-start.3
  0.7 18.5 %shard_map.82 = (s32[8,8,128]{2,1,0:T(8,128)}, bf16[2,256,256]{2,1,0:T(8,128)(2,1)}, bf16[4,256,256]{2,1,0:T(8,128)(2,1)}) custom-call(s32[1]{0:T(128)S(6)} %copy.9.point_ref, s32[64,256]{1,0:T(8,128)} %mask_ref.1, f32[64,256]{1,0:T(8,128)} %phase_ref.1, bf16[4,32,256]{2,1,0:T(8,128)(2,1)} %modes_ref.1), custom_call_target="tpu_custom_call" | custom-call | tf_op jit(solution)/shard_map/pallas_call | solution.py:248
  19.2 0.0 copy-start.6
  19.2 0.0 copy-done.3
  19.2 0.6 %copy-done.6 = s32[8]{0:T(128)S(1)} copy-done((s32[8]{0:T(128)S(1)}, s32[8]{0:T(128)}, u32[]{:S(2)}) %copy-start.6) | copy-done | bytes 56
  19.8 0.0 copy-start
  19.8 1.0 %copy-done = bf16[4,256,256]{2,1,0:T(8,128)(2,1)S(1)} copy-done((bf16[4,256,256]{2,1,0:T(8,128)(2,1)S(1)}, bf16[4,256,256]{2,1,0:T(8,128)(2,1)}, u32[]{:S(2)}) %copy-start) | copy-done | bytes 524312
  20.9 0.0 copy-start.1
  20.9 0.9 %copy-done.1 = f32[256,256]{1,0:T(8,128)S(1)} copy-done((f32[256,256]{1,0:T(8,128)S(1)}, f32[256,256]{1,0:T(8,128)}, u32[]{:S(2)}) %copy-start.1) | copy-done | bytes 262168
  21.8 0.0 copy-start.2
  21.8 0.9 %copy-done.2 = bf16[2,256,256]{2,1,0:T(8,128)(2,1)S(1)} copy-done((bf16[2,256,256]{2,1,0:T(8,128)(2,1)S(1)}, bf16[2,256,256]{2,1,0:T(8,128)(2,1)}, u32[]{:S(2)}) %copy-start.2) | copy-done | bytes 262168
  22.8 0.0 copy-start.4
  22.8 0.9 %copy-done.4 = bf16[256,256]{1,0:T(8,128)(2,1)S(1)} copy-done((bf16[256,256]{1,0:T(8,128)(2,1)S(1)}, bf16[256,256]{1,0:T(8,128)(2,1)}, u32[]{:S(2)}) %copy-start.4) | copy-done | bytes 131096
  23.7 0.0 copy-start.5
  23.7 0.8 %copy-done.5 = s32[8,8,128]{2,1,0:T(8,128)S(1)} copy-done((s32[8,8,128]{2,1,0:T(8,128)S(1)}, s32[8,8,128]{2,1,0:T(8,128)}, u32[]{:S(2)}) %copy-start.5) | copy-done | bytes 32792
  24.4 6.5 %shard_map.83 = f32[64,4,512]{2,1,0:T(4,128)} custom-call(s32[8]{0:T(128)S(1)} %copy-done.6, s32[8,8,128]{2,1,0:T(8,128)S(1)} %copy-done.5, f32[256,256]{1,0:T(8,128)S(1)} %copy-done.1, bf16[2,256,256]{2,1,0:T(8,128)(2,1)S(1)} %copy-done.2, bf16[4,256,256]{2,1,0:T(8,128)(2,1)S(1)} %copy-done, bf16[256,256]{1,0:T(8,128)(2,1)S(1)} %copy-done.4, ...), custom_call_target="tpu_custom_call" | custom-call | tf_op jit(solution)/shard_map/pallas_call | solution.py:278
Async XLA Ops:
  0.0 19.2 %copy-start.3 = (bf16[256,256]{1,0:T(8,128)(2,1)S(1)}, bf16[256,256]{1,0:T(8,128)(2,1)}, u32[]{:S(2)}) copy-start(bf16[256,256]{1,0:T(8,128)(2,1)} %constant.8.clone.flip_ref) | copy-start | bytes 393220
  19.2 0.7 %copy-start.6 = (s32[8]{0:T(128)S(1)}, s32[8]{0:T(128)}, u32[]{:S(2)}) copy-start(s32[8]{0:T(128)} %blocks_ref.1) | copy-start | bytes 100
  19.8 1.0 %copy-start = (bf16[4,256,256]{2,1,0:T(8,128)(2,1)S(1)}, bf16[4,256,256]{2,1,0:T(8,128)(2,1)}, u32[]{:S(2)}) copy-start(bf16[4,256,256]{2,1,0:T(8,128)(2,1)} %get-tuple-element.10.modes_ref) | copy-start | bytes 1572868
  20.9 0.9 %copy-start.1 = (f32[256,256]{1,0:T(8,128)S(1)}, f32[256,256]{1,0:T(8,128)}, u32[]{:S(2)}) copy-start(f32[256,256]{1,0:T(8,128)} %constant.6.clone.rows_ref) | copy-start | bytes 786436
  21.8 0.9 %copy-start.2 = (bf16[2,256,256]{2,1,0:T(8,128)(2,1)S(1)}, bf16[2,256,256]{2,1,0:T(8,128)(2,1)}, u32[]{:S(2)}) copy-start(bf16[2,256,256]{2,1,0:T(8,128)(2,1)} %get-tuple-element.9.field_ref) | copy-start | bytes 786436
  22.8 0.9 %copy-start.4 = (bf16[256,256]{1,0:T(8,128)(2,1)S(1)}, bf16[256,256]{1,0:T(8,128)(2,1)}, u32[]{:S(2)}) copy-start(bf16[256,256]{1,0:T(8,128)(2,1)} %constant.7.clone.hilbert_ref) | copy-start | bytes 393220
  23.7 0.8 %copy-start.5 = (s32[8,8,128]{2,1,0:T(8,128)S(1)}, s32[8,8,128]{2,1,0:T(8,128)}, u32[]{:S(2)}) copy-start(s32[8,8,128]{2,1,0:T(8,128)} %get-tuple-element.8.points_ref) | copy-start | bytes 98308

commit v3 on v1

--- a/solution.py
+++ b/solution.py
@@ -28,23 +28,161 @@
     flip = np.zeros((pupil, pupil))
     flip[mirror, np.arange(pupil)] = 1.0
     return (
-        whole.real.astype(np.float32),
-        whole.imag.astype(np.float32),
+        whole.imag[:pupil].astype(np.float32),
         hilbert.astype(jnp.bfloat16),
         flip.astype(jnp.bfloat16),
     )
 
 
 def tangent_kernel(
-    factor, block_ref, points_ref, rows_re_ref, rows_im_ref, field_ref, modes_ref, hilbert_ref,
-    flip_ref, out_ref, left_ref, weight_ref, rot_ref, bent_ref, wide_ref, own_ref, acc_ref,
+    factor, count_y, point_ref, blocks_ref, mask_hbm, phase_hbm, modes_hbm, rows_hbm, hilbert_hbm,
+    flip_hbm, out_ref, points_ref, field_ref, values_ref, own_point, own_field, mask_ref, phase_ref,
+    rows_ref, hilbert_ref, flip_ref, left_ref, weight_ref, rot_ref, bent_ref, wide_ref, own_ref,
+    local_sem, point_send, point_recv, field_send, field_recv, z_send, z_recv, relay_send, y_send,
+    y_recv,
 ):
-    mods, pupil = points_ref.shape
-    rows = rows_re_ref.shape[0]
-    mode_dev = modes_ref.shape[0]
+    mod_count = lax.axis_size("mod")
+    mode_count = lax.axis_size("mode")
+    count_z = mod_count // count_y
+    me, mine = lax.axis_index("mod"), lax.axis_index("mode")
+    y, z = lax.rem(me, count_y), me // count_y
+    mode_dev, share, pupil = modes_hbm.shape
+    stripe = mask_ref.shape[0]
+    mods = mod_count
+    rows = out_ref.shape[0]
     f32 = jnp.float32
     bf16 = jnp.bfloat16
-    theta = points_ref[...].astype(f32) * (2.0 * math.pi / NPTS)
+    mesh = pl.DeviceIdType.MESH
+    along_z = [lax.rem(z + d, count_z) * count_y + y for d in range(1, count_z)]
+    from_z = [lax.rem(z + count_z - d, count_z) * count_y + y for d in range(1, count_z)]
+    along_y = [z * count_y + lax.rem(y + d, count_y) for d in range(1, count_y)]
+    beside = [lax.rem(mine + d, mode_count) for d in range(1, mode_count)]
+    relayed = count_z == 4
+
+    early = [
+        pltpu.make_async_copy(mask_hbm, mask_ref, local_sem.at[0]),
+        pltpu.make_async_copy(phase_hbm, phase_ref, local_sem.at[1]),
+    ]
+    tables = [
+        pltpu.make_async_copy(rows_hbm, rows_ref, local_sem.at[2]),
+        pltpu.make_async_copy(hilbert_hbm, hilbert_ref, local_sem.at[3]),
+        pltpu.make_async_copy(flip_hbm, flip_ref, local_sem.at[4]),
+    ]
+    barrier = pltpu.get_barrier_semaphore()
+    for peer in along_z + along_y:
+        pl.semaphore_signal(barrier, inc=1, device_id=(peer, mine), device_id_type=mesh)
+    for peer in beside:
+        pl.semaphore_signal(barrier, inc=1, device_id=(me, peer), device_id_type=mesh)
+    for copy in early + tables:
+        copy.start()
+
+    own_point[...] = jnp.full(own_point.shape, point_ref[0], jnp.int32)
+    for copy in early:
+        copy.wait()
+    mask = mask_ref[...].astype(f32)
+    own_field[0] = (mask * jnp.cos(phase_ref[...])).astype(bf16)
+    own_field[1] = (mask * jnp.sin(phase_ref[...])).astype(bf16)
+    pl.semaphore_wait(barrier, len(along_z) + len(along_y) + len(beside))
+
+    def lines(i):
+        return pl.ds(pl.multiple_of(i * share, share), share)
+
+    def make(source, target, sent, landed, peer):
+        return pltpu.make_async_remote_copy(
+            src_ref=source, dst_ref=target, send_sem=sent, recv_sem=landed,
+            device_id=peer, device_id_type=mesh,
+        )
+
+    def send(*args):
+        copy = make(*args)
+        copy.start()
+        return copy
+
+    copies = []
+    for d, peer in enumerate(along_z):
+        copies.append(
+            send(own_point, points_ref.at[me], point_send.at[d], point_recv.at[d], (peer, mine))
+        )
+    for d, peer in enumerate(along_y):
+        copies.append(
+            send(
+                own_point, points_ref.at[me], point_send.at[count_z - 1 + d],
+                point_recv.at[count_z - 1 + d], (peer, mine),
+            )
+        )
+    held = pl.ds(pl.multiple_of(mine * stripe, stripe), stripe)
+    field_copies = [
+        send(own_field, field_ref.at[:, held], field_send.at[d], field_recv.at[d], (me, peer))
+        for d, peer in enumerate(beside)
+    ]
+
+    def ends(d):
+        if not relayed or d == 1:
+            return None
+        return count_z - 1 if d == 0 else 0
+
+    order = [1, 0, 2] if relayed else list(range(count_z - 1))
+    z_copies = []
+    y_copies = []
+    relays = []
+    for j in range(mode_dev):
+        here = values_ref.at[j, lines(me)]
+        row = [
+            make(modes_hbm.at[j], here, z_send.at[j, d], z_recv.at[j, d], (peer, mine))
+            for d, peer in enumerate(along_z)
+        ]
+        for d in order:
+            if ends(d) is None:
+                row[d].start()
+            else:
+                pl.when(z != ends(d))(row[d].start)
+        z_copies.append(row)
+        y_copies.append([
+            send(modes_hbm.at[j], here, y_send.at[j, 0, d], y_recv.at[j, 0, d], (peer, mine))
+            for d, peer in enumerate(along_y)
+        ])
+        if relayed:
+            piece = values_ref.at[j, lines(from_z[1])]
+            relays.append([
+                make(piece, piece, relay_send.at[j], z_recv.at[j, 0], (y, mine)),
+                make(piece, piece, relay_send.at[j], z_recv.at[j, 2], (3 * count_y + y, mine)),
+            ])
+    stay = [
+        pltpu.make_async_copy(own_point, points_ref.at[me], local_sem.at[5]),
+        pltpu.make_async_copy(own_field, field_ref.at[:, held], local_sem.at[6]),
+        pltpu.make_async_copy(modes_hbm, values_ref.at[:, lines(me)], local_sem.at[7]),
+    ]
+    for copy in stay:
+        copy.start()
+
+    for d, source in enumerate(from_z):
+        copies[d].wait_recv()
+        for e, peer in enumerate(along_y):
+            at = count_z - 1 + (d + 1) * len(along_y) + e
+            copies.append(
+                send(
+                    points_ref.at[source], points_ref.at[source], point_send.at[at],
+                    point_recv.at[at], (peer, mine),
+                )
+            )
+
+    def forward(j):
+        for d in order:
+            z_copies[j][d].wait_recv()
+            if relayed and d == 1:
+                pl.when(z == 1)(relays[j][0].start)
+                pl.when(z == 2)(relays[j][1].start)
+            piece = values_ref.at[j, lines(from_z[d])]
+            for e, peer in enumerate(along_y):
+                y_copies[j].append(
+                    send(piece, piece, y_send.at[j, d + 1, e], y_recv.at[j, d + 1, e], (peer, mine))
+                )
+
+    for copy in tables + stay:
+        copy.wait()
+    for copy in copies[count_z - 1 :]:
+        copy.wait_recv()
+    theta = points_ref[...][:, 0, :1].astype(f32) * (2.0 * math.pi / NPTS)
     centred = (lax.broadcasted_iota(jnp.int32, (mods, pupil), 1) - pupil // 2).astype(f32)
     scale = 2.0 * math.pi * radius_cells / (2 * pupil)
     row_angle = scale * jnp.cos(theta) * centred
@@ -52,8 +190,19 @@
     row_cos, row_sin = jnp.cos(row_angle), jnp.sin(row_angle)
     rot_ref[0] = jnp.cos(col_angle)
     rot_ref[1] = jnp.sin(col_angle)
-    rows_re = rows_re_ref[...]
-    rows_im = rows_im_ref[...]
+    block = blocks_ref[me]
+    place = lax.broadcasted_iota(jnp.int32, (rows, pupil), 0) + lax.broadcasted_iota(
+        jnp.int32, (rows, pupil), 1
+    )
+    rows_re = jnp.zeros((rows, pupil), f32)
+    rows_im = jnp.zeros((rows, pupil), f32)
+    for b in range(blocks_ref.shape[0]):
+        chosen = (jnp.full((1, pupil), block, jnp.int32) == b).astype(f32)
+        start = b * rows % pupil
+        facing = ((place + start) % pupil == 0).astype(f32)
+        sign = 1.0 if b * rows < pupil else -1.0
+        rows_re += 0.5 * chosen * facing
+        rows_im += sign * chosen * rows_ref[start : start + rows]
     for k in range(mods):
         cos, sin = row_cos[k : k + 1], row_sin[k : k + 1]
         re = (rows_re * cos - rows_im * sin).astype(bf16)
@@ -107,67 +256,98 @@
                 )
                 out_ref[:, mode, half * pupil : (half + 1) * pupil] = placed
 
+    forward(0)
+    if mode_dev > 1:
+        forward(1)
+    for copy in field_copies:
+        copy.wait_recv()
     weight_ref[:pupil] = field_ref[0]
     weight_ref[pupil:] = field_ref[1]
     detector(True, 0)
+    for mode in range(2, mode_dev):
+        forward(mode)
     for mode in range(mode_dev):
-        values = modes_ref[mode].astype(f32)
+        for copy in y_copies[mode]:
+            copy.wait_recv()
+        values = values_ref[mode].astype(f32)
         weight_ref[:pupil] = (-values * field_ref[1].astype(f32)).astype(bf16)
         weight_ref[pupil:] = (values * field_ref[0].astype(f32)).astype(bf16)
         detector(False, mode)
-
-
-def tangent_call(block, points, field, modes, factor, rows, mods):
-    mode_dev, pupil, _ = modes.shape
-    rows_re, rows_im, hilbert, flip = operator_tables(pupil)
-    whole = lambda *shape: pl.BlockSpec(shape, lambda i, b: (0,) * len(shape))
-    picked = pl.BlockSpec((rows, pupil), lambda i, b: (b[0], 0))
-    spec = pltpu.PrefetchScalarGridSpec(
-        num_scalar_prefetch=1,
-        grid=(1,),
-        in_specs=[
-            whole(mods, pupil),
-            picked,
-            picked,
-            whole(2, pupil, pupil),
-            whole(mode_dev, pupil, pupil),
-            whole(pupil, pupil),
-            whole(pupil, pupil),
+    for copy in copies + field_copies + sum(y_copies, []):
+        copy.wait_send()
+    for j in range(mode_dev):
+        for d in range(count_z - 1):
+            if ends(d) is None:
+                z_copies[j][d].wait_send()
+            else:
+                pl.when(z != ends(d))(z_copies[j][d].wait_send)
+        if relayed:
+            pl.when(z == 1)(relays[j][0].wait_send)
+            pl.when(z == 2)(relays[j][1].wait_send)
+
+
+def tangent_call(mod_points, pupil_mask, phase_offset, modes, block_map, factor):
+    mod_count = lax.axis_size("mod")
+    mode_count = lax.axis_size("mode")
+    mode_dev, share, pupil = modes.shape
+    stripe = pupil_mask.shape[0]
+    rows = 2 * pupil // block_map.shape[0]
+    count_y = 2 if mod_count % 2 == 0 else 1
+    count_z = mod_count // count_y
+    below, hilbert, flip = operator_tables(pupil)
+    smem = pl.BlockSpec(memory_space=pltpu.SMEM)
+    away = pl.BlockSpec(memory_space=pl.ANY)
+    dma = pltpu.SemaphoreType.DMA
+    few = max(count_y - 1, 1)
+    points = count_z - 1 + count_z * few
+    tall = 2 * rows * mod_count
+    bf16 = jnp.bfloat16
+    f32 = jnp.float32
+    return pl.pallas_call(
+        functools.partial(tangent_kernel, factor, count_y),
+        in_specs=[smem, smem] + [away] * 6,
+        out_specs=pl.BlockSpec(memory_space=pltpu.VMEM),
+        out_shape=jax.ShapeDtypeStruct((rows, mode_dev, 2 * pupil), f32),
+        scratch_shapes=[
+            pltpu.VMEM((mod_count, 8, 128), jnp.int32),
+            pltpu.VMEM((2, pupil, pupil), bf16),
+            pltpu.VMEM((mode_dev, pupil, pupil), bf16),
+            pltpu.VMEM((8, 128), jnp.int32),
+            pltpu.VMEM((2, stripe, pupil), bf16),
+            pltpu.VMEM((stripe, pupil), jnp.int32),
+            pltpu.VMEM((stripe, pupil), f32),
+            pltpu.VMEM((pupil, pupil), f32),
+            pltpu.VMEM((pupil, pupil), bf16),
+            pltpu.VMEM((pupil, pupil), bf16),
+            pltpu.VMEM((tall, 2 * pupil), bf16),
+            pltpu.VMEM((2 * pupil, pupil), bf16),
+            pltpu.VMEM((2, mod_count, pupil), f32),
+            pltpu.VMEM((tall, pupil), bf16),
+            pltpu.VMEM((tall, pupil), f32),
+            pltpu.VMEM((mod_count, 4, rows, pupil), f32),
+            dma((8,)),
+            dma((points,)),
+            dma((points,)),
+            dma((mode_count - 1,)),
+            dma((mode_count - 1,)),
+            dma((mode_dev, count_z - 1)),
+            dma((mode_dev, count_z - 1)),
+            dma((mode_dev,)),
+            dma((mode_dev, count_z, few)),
+            dma((mode_dev, count_z, few)),
         ],
-        out_specs=whole(rows, mode_dev, 2 * pupil),
-        scratch_shapes=[
-            pltpu.VMEM((2 * rows * mods, 2 * pupil), jnp.bfloat16),
-            pltpu.VMEM((2 * pupil, pupil), jnp.bfloat16),
-            pltpu.VMEM((2, mods, pupil), jnp.float32),
-            pltpu.VMEM((2 * rows * mods, pupil), jnp.bfloat16),
-            pltpu.VMEM((2 * rows * mods, pupil), jnp.float32),
-            pltpu.VMEM((mods, 4, rows, pupil), jnp.float32),
-            pltpu.VMEM((rows, pupil), jnp.float32),
-        ],
-    )
-    return pl.pallas_call(
-        functools.partial(tangent_kernel, factor),
-        grid_spec=spec,
-        out_shape=jax.ShapeDtypeStruct((rows, mode_dev, 2 * pupil), jnp.float32),
-        compiler_params=pltpu.CompilerParams(vmem_limit_bytes=48 * 1024 * 1024),
-    )(block, points, rows_re, rows_im, field, modes, hilbert, flip)
+        compiler_params=pltpu.CompilerParams(
+            collective_id=0, has_side_effects=True, vmem_limit_bytes=60 * 1024 * 1024
+        ),
+    )(mod_points, block_map, pupil_mask, phase_offset, modes, below, hilbert, flip)
 
 
 def local(mod_points, pupil_mask, phase_offset, modes, block_map):
-    mod_count = lax.axis_size("mod")
-    mods = mod_points.shape[0] * mod_count
+    mods = mod_points.shape[0] * lax.axis_size("mod")
     pupil = modes.shape[2]
     length = 2 * pupil
-    rows = length // block_map.shape[0]
-    mask = pupil_mask.astype(jnp.float32)
-    own = jnp.stack([mask * jnp.cos(phase_offset), mask * jnp.sin(phase_offset)])
-    field = lax.all_gather(own.astype(jnp.bfloat16), "mode", axis=1, tiled=True)
-    values = lax.all_gather(modes, "mod", axis=1, tiled=True)
-    points = lax.all_gather(mod_points, "mod", axis=0, tiled=True)
-    points = jnp.broadcast_to(points[:, None], (mods, pupil))
-    block = lax.dynamic_slice(block_map, (lax.axis_index("mod"),), (1,))
     factor = 2.0 * 0.25 * float(length * length) / float(pupil * pupil * mods)
-    return tangent_call(block, points, field, values, factor, rows, mods)
+    return tangent_call(mod_points, pupil_mask, phase_offset, modes, block_map, factor)
 
 
 def solution(mesh):

time: 62.5 us -> 26.3 us (0.42)
  blocking collectives: 50.5 us -> 0 us
  Pallas kernels: 6.33 us -> 23.6 us
  local copies, waits for them, and re-layouts: 3.57 us -> 1.87 us
  other arithmetic: 1.16 us -> 0 us
    all_gather x2 -> x0, blocking collectives: 37.4 us -> none  [the longest x1 31.5 us: local(): values = lax.all_gather(modes, 'mod', axis=1, tiled=True)]
    pallas_call x1, Pallas kernels: 6.33 us -> 23.6 us  [tangent_call(): pl.pallas_call(functools.partial(tangent_kernel, factor, count_y), in_spe...]
    unnamed x1 -> x0, blocking collectives: 13.1 us -> none
    another operation x2 -> x0, other arithmetic: 1.16 us -> none  [local(): jnp.stack([mask * jnp.cos(phase_offset), mask * jnp.sin(phase_offset)])]
    unnamed x17 -> x1, local copies, waits for them, and re-layouts: 2.92 us -> 1.87 us
where the time goes in v3:
time: 26.3 us; the launch traced here: 26.1 us
  Pallas kernels  23.6 us (90%)
  local copies, waits for them, and re-layouts  1.87 us (7%)
  between operations  0.66 us (3%)
    pallas_call x1, Pallas kernels, tangent_call(): pl.pallas_call(functools.partial(tangent_kernel, factor, count_y), in_spe...  23.6 us
    unnamed x1, local copies, waits for them, and re-layouts  1.87 us

profile of v3, /device:TPU:0, one launch (start us, length us, event | category | flops | bytes accessed | tf_op | source)
XLA Modules:
  0.0 26.1 jit_solution(6988898344758966701)
XLA Ops:
  0.7 23.6 %shard_map.82 = f32[64,4,512]{2,1,0:T(4,128)} custom-call(s32[1]{0:T(128)S(6)} %copy.10.point_ref, s32[8]{0:T(128)} %blocks_ref.1, s32[64,256]{1,0:T(8,128)} %mask_hbm.1, f32[64,256]{1,0:T(8,128)} %phase_hbm.1, bf16[4,32,256]{2,1,0:T(8,128)(2,1)} %modes_hbm.1, f32[256,256]{1,0:T(8,128)} %constant.6.clone.rows_hbm, ...), custom_call_target="tpu_custom_call" | custom-call | tf_op jit(solution)/shard_map/pallas_call | solution.py:306
  24.3 1.9 %copy.11 = f32[64,4,512]{2,1,0:T(4,128)} copy(f32[64,4,512]{2,1,0:T(4,128)} %shard_map.82) | data formatting | bytes 1048576

commit v4 on v3

--- a/solution.py
+++ b/solution.py
@@ -38,7 +38,7 @@
     factor, count_y, point_ref, blocks_ref, mask_hbm, phase_hbm, modes_hbm, rows_hbm, hilbert_hbm,
     flip_hbm, out_ref, points_ref, field_ref, values_ref, own_point, own_field, mask_ref, phase_ref,
     rows_ref, hilbert_ref, flip_ref, left_ref, weight_ref, rot_ref, bent_ref, wide_ref, own_ref,
-    local_sem, point_send, point_recv, field_send, field_recv, z_send, z_recv, relay_send, y_send,
+    local_sem, point_send, point_recv, field_send, field_recv, z_send, z_recv, y_send,
     y_recv,
 ):
     mod_count = lax.axis_size("mod")
@@ -57,7 +57,6 @@
     from_z = [lax.rem(z + count_z - d, count_z) * count_y + y for d in range(1, count_z)]
     along_y = [z * count_y + lax.rem(y + d, count_y) for d in range(1, count_y)]
     beside = [lax.rem(mine + d, mode_count) for d in range(1, mode_count)]
-    relayed = count_z == 4
 
     early = [
         pltpu.make_async_copy(mask_hbm, mask_ref, local_sem.at[0]),
@@ -87,14 +86,11 @@
     def lines(i):
         return pl.ds(pl.multiple_of(i * share, share), share)
 
-    def make(source, target, sent, landed, peer):
-        return pltpu.make_async_remote_copy(
+    def send(source, target, sent, landed, peer):
+        copy = pltpu.make_async_remote_copy(
             src_ref=source, dst_ref=target, send_sem=sent, recv_sem=landed,
             device_id=peer, device_id_type=mesh,
         )
-
-    def send(*args):
-        copy = make(*args)
         copy.start()
         return copy
 
@@ -116,37 +112,18 @@
         for d, peer in enumerate(beside)
     ]
 
-    def ends(d):
-        if not relayed or d == 1:
-            return None
-        return count_z - 1 if d == 0 else 0
-
-    order = [1, 0, 2] if relayed else list(range(count_z - 1))
     z_copies = []
     y_copies = []
-    relays = []
     for j in range(mode_dev):
         here = values_ref.at[j, lines(me)]
-        row = [
-            make(modes_hbm.at[j], here, z_send.at[j, d], z_recv.at[j, d], (peer, mine))
+        z_copies.append([
+            send(modes_hbm.at[j], here, z_send.at[j, d], z_recv.at[j, d], (peer, mine))
             for d, peer in enumerate(along_z)
-        ]
-        for d in order:
-            if ends(d) is None:
-                row[d].start()
-            else:
-                pl.when(z != ends(d))(row[d].start)
-        z_copies.append(row)
+        ])
         y_copies.append([
             send(modes_hbm.at[j], here, y_send.at[j, 0, d], y_recv.at[j, 0, d], (peer, mine))
             for d, peer in enumerate(along_y)
         ])
-        if relayed:
-            piece = values_ref.at[j, lines(from_z[1])]
-            relays.append([
-                make(piece, piece, relay_send.at[j], z_recv.at[j, 0], (y, mine)),
-                make(piece, piece, relay_send.at[j], z_recv.at[j, 2], (3 * count_y + y, mine)),
-            ])
     stay = [
         pltpu.make_async_copy(own_point, points_ref.at[me], local_sem.at[5]),
         pltpu.make_async_copy(own_field, field_ref.at[:, held], local_sem.at[6]),
@@ -167,11 +144,8 @@
             )
 
     def forward(j):
-        for d in order:
+        for d in range(count_z - 1):
             z_copies[j][d].wait_recv()
-            if relayed and d == 1:
-                pl.when(z == 1)(relays[j][0].start)
-                pl.when(z == 2)(relays[j][1].start)
             piece = values_ref.at[j, lines(from_z[d])]
             for e, peer in enumerate(along_y):
                 y_copies[j].append(
@@ -273,17 +247,8 @@
         weight_ref[:pupil] = (-values * field_ref[1].astype(f32)).astype(bf16)
         weight_ref[pupil:] = (values * field_ref[0].astype(f32)).astype(bf16)
         detector(False, mode)
-    for copy in copies + field_copies + sum(y_copies, []):
+    for copy in copies + field_copies + sum(z_copies, []) + sum(y_copies, []):
         copy.wait_send()
-    for j in range(mode_dev):
-        for d in range(count_z - 1):
-            if ends(d) is None:
-                z_copies[j][d].wait_send()
-            else:
-                pl.when(z != ends(d))(z_copies[j][d].wait_send)
-        if relayed:
-            pl.when(z == 1)(relays[j][0].wait_send)
-            pl.when(z == 2)(relays[j][1].wait_send)
 
 
 def tangent_call(mod_points, pupil_mask, phase_offset, modes, block_map, factor):
@@ -332,7 +297,6 @@
             dma((mode_count - 1,)),
             dma((mode_dev, count_z - 1)),
             dma((mode_dev, count_z - 1)),
-            dma((mode_dev,)),
             dma((mode_dev, count_z, few)),
             dma((mode_dev, count_z, few)),
         ],

time: 26.3 us -> 24.4 us (0.928)
  Pallas kernels: 23.6 us -> 21.7 us
    pallas_call x1, Pallas kernels: 23.6 us -> 21.7 us  [tangent_call(): pl.pallas_call(functools.partial(tangent_kernel, factor, count_y), in_spe...]
where the time goes in v4:
time: 24.4 us; the launch traced here: 24.2 us
  Pallas kernels  21.7 us (89%)
  local copies, waits for them, and re-layouts  1.87 us (8%)
  between operations  0.66 us (3%)
    pallas_call x1, Pallas kernels, tangent_call(): pl.pallas_call(functools.partial(tangent_kernel, factor, count_y), in_spe...  21.7 us
    unnamed x1, local copies, waits for them, and re-layouts  1.87 us

profile of v4, /device:TPU:0, one launch (start us, length us, event | category | flops | bytes accessed | tf_op | source)
XLA Modules:
  0.0 24.2 jit_solution(14902078567500768031)
XLA Ops:
  0.7 21.7 %shard_map.82 = f32[64,4,512]{2,1,0:T(4,128)} custom-call(s32[1]{0:T(128)S(6)} %copy.10.point_ref, s32[8]{0:T(128)} %blocks_ref.1, s32[64,256]{1,0:T(8,128)} %mask_hbm.1, f32[64,256]{1,0:T(8,128)} %phase_hbm.1, bf16[4,32,256]{2,1,0:T(8,128)(2,1)} %modes_hbm.1, f32[256,256]{1,0:T(8,128)} %constant.6.clone.rows_hbm, ...), custom_call_target="tpu_custom_call" | custom-call | tf_op jit(solution)/shard_map/pallas_call | solution.py:271
  22.3 1.9 %copy.11 = f32[64,4,512]{2,1,0:T(4,128)} copy(f32[64,4,512]{2,1,0:T(4,128)} %shard_map.82) | data formatting | bytes 1048576

commit v5 on v4

--- a/solution.py
+++ b/solution.py
@@ -36,8 +36,8 @@
 
 def tangent_kernel(
     factor, count_y, point_ref, blocks_ref, mask_hbm, phase_hbm, modes_hbm, rows_hbm, hilbert_hbm,
-    flip_hbm, out_ref, points_ref, field_ref, values_ref, own_point, own_field, mask_ref, phase_ref,
-    rows_ref, hilbert_ref, flip_ref, left_ref, weight_ref, rot_ref, bent_ref, wide_ref, own_ref,
+    out_ref, points_ref, field_ref, values_ref, own_point, own_field, mask_ref, phase_ref,
+    rows_ref, hilbert_ref, left_ref, weight_ref, rot_ref, bent_ref, wide_ref, own_ref,
     local_sem, point_send, point_recv, field_send, field_recv, z_send, z_recv, y_send,
     y_recv,
 ):
@@ -49,7 +49,7 @@
     mode_dev, share, pupil = modes_hbm.shape
     stripe = mask_ref.shape[0]
     mods = mod_count
-    rows = out_ref.shape[0]
+    rows = out_ref.shape[3]
     f32 = jnp.float32
     bf16 = jnp.bfloat16
     mesh = pl.DeviceIdType.MESH
@@ -65,7 +65,6 @@
     tables = [
         pltpu.make_async_copy(rows_hbm, rows_ref, local_sem.at[2]),
         pltpu.make_async_copy(hilbert_hbm, hilbert_ref, local_sem.at[3]),
-        pltpu.make_async_copy(flip_hbm, flip_ref, local_sem.at[4]),
     ]
     barrier = pltpu.get_barrier_semaphore()
     for peer in along_z + along_y:
@@ -225,10 +224,8 @@
                 total = total * factor
                 coarse = total.astype(bf16)
                 fine = (total - coarse.astype(f32)).astype(bf16)
-                placed = jnp.dot(coarse, flip_ref[...], preferred_element_type=f32) + jnp.dot(
-                    fine, flip_ref[...], preferred_element_type=f32
-                )
-                out_ref[:, mode, half * pupil : (half + 1) * pupil] = placed
+                out_ref[mode, 0, half] = coarse
+                out_ref[mode, 1, half] = fine
 
     forward(0)
     if mode_dev > 1:
@@ -259,7 +256,7 @@
     rows = 2 * pupil // block_map.shape[0]
     count_y = 2 if mod_count % 2 == 0 else 1
     count_z = mod_count // count_y
-    below, hilbert, flip = operator_tables(pupil)
+    below, hilbert, _ = operator_tables(pupil)
     smem = pl.BlockSpec(memory_space=pltpu.SMEM)
     away = pl.BlockSpec(memory_space=pl.ANY)
     dma = pltpu.SemaphoreType.DMA
@@ -270,9 +267,9 @@
     f32 = jnp.float32
     return pl.pallas_call(
         functools.partial(tangent_kernel, factor, count_y),
-        in_specs=[smem, smem] + [away] * 6,
+        in_specs=[smem, smem] + [away] * 5,
         out_specs=pl.BlockSpec(memory_space=pltpu.VMEM),
-        out_shape=jax.ShapeDtypeStruct((rows, mode_dev, 2 * pupil), f32),
+        out_shape=jax.ShapeDtypeStruct((mode_dev, 2, 2, rows, pupil), bf16),
         scratch_shapes=[
             pltpu.VMEM((mod_count, 8, 128), jnp.int32),
             pltpu.VMEM((2, pupil, pupil), bf16),
@@ -282,7 +279,6 @@
             pltpu.VMEM((stripe, pupil), jnp.int32),
             pltpu.VMEM((stripe, pupil), f32),
             pltpu.VMEM((pupil, pupil), f32),
-            pltpu.VMEM((pupil, pupil), bf16),
             pltpu.VMEM((pupil, pupil), bf16),
             pltpu.VMEM((tall, 2 * pupil), bf16),
             pltpu.VMEM((2 * pupil, pupil), bf16),
@@ -303,7 +299,32 @@
         compiler_params=pltpu.CompilerParams(
             collective_id=0, has_side_effects=True, vmem_limit_bytes=60 * 1024 * 1024
         ),
-    )(mod_points, block_map, pupil_mask, phase_offset, modes, below, hilbert, flip)
+    )(mod_points, block_map, pupil_mask, phase_offset, modes, below, hilbert)
+
+
+def mirror_kernel(parts_ref, flip_ref, out_ref):
+    mode_dev, _, halves, _, pupil = parts_ref.shape
+    for mode in range(mode_dev):
+        for half in range(halves):
+            coarse = jnp.dot(
+                parts_ref[mode, 0, half], flip_ref[...], preferred_element_type=jnp.float32
+            )
+            fine = jnp.dot(
+                parts_ref[mode, 1, half], flip_ref[...], preferred_element_type=jnp.float32
+            )
+            out_ref[:, mode, half * pupil : (half + 1) * pupil] = coarse + fine
+
+
+def mirror_call(parts):
+    mode_dev, _, halves, rows, pupil = parts.shape
+    flip = operator_tables(pupil)[2]
+    vmem = pl.BlockSpec(memory_space=pltpu.VMEM)
+    return pl.pallas_call(
+        mirror_kernel,
+        in_specs=[vmem, vmem],
+        out_specs=vmem,
+        out_shape=jax.ShapeDtypeStruct((rows, mode_dev, halves * pupil), jnp.float32),
+    )(parts, flip)
 
 
 def local(mod_points, pupil_mask, phase_offset, modes, block_map):
@@ -311,7 +332,8 @@
     pupil = modes.shape[2]
     length = 2 * pupil
     factor = 2.0 * 0.25 * float(length * length) / float(pupil * pupil * mods)
-    return tangent_call(mod_points, pupil_mask, phase_offset, modes, block_map, factor)
+    parts = tangent_call(mod_points, pupil_mask, phase_offset, modes, block_map, factor)
+    return mirror_call(parts)
 
 
 def solution(mesh):

time: 24.4 us -> 24 us (0.984)
  local copies, waits for them, and re-layouts: 1.87 us -> 0 us
  Pallas kernels: 21.7 us -> 23.2 us
    pallas_call x0 -> x1, Pallas kernels: none -> 2.38 us  [mirror_call(): pl.pallas_call(mirror_kernel, in_specs=[vmem, vmem], out_specs=vmem, out_...]
    unnamed x1 -> x0, local copies, waits for them, and re-layouts: 1.87 us -> none
    pallas_call x1, Pallas kernels: 21.7 us -> 20.8 us  [tangent_call(): pl.pallas_call(functools.partial(tangent_kernel, factor, count_y), in_spe...]
where the time goes in v5:
time: 24 us; the launch traced here: 23.8 us
  Pallas kernels  23.2 us (97%)
  between operations  0.66 us (3%)
    pallas_call x1, Pallas kernels, tangent_call(): pl.pallas_call(functools.partial(tangent_kernel, factor, count_y), in_spe...  20.8 us
    pallas_call x1, Pallas kernels, mirror_call(): pl.pallas_call(mirror_kernel, in_specs=[vmem, vmem], out_specs=vmem, out_...  2.38 us

profile of v5, /device:TPU:0, one launch (start us, length us, event | category | flops | bytes accessed | tf_op | source)
XLA Modules:
  0.0 23.8 jit_solution(2912481952541888863)
XLA Ops:
  0.7 20.8 %shard_map.82.parts_ref = bf16[4,2,2,64,256]{4,3,2,1,0:T(8,128)(2,1)} custom-call(s32[1]{0:T(128)S(6)} %copy.9.point_ref, s32[8]{0:T(128)} %blocks_ref.1, s32[64,256]{1,0:T(8,128)} %mask_hbm.1, f32[64,256]{1,0:T(8,128)} %phase_hbm.1, bf16[4,32,256]{2,1,0:T(8,128)(2,1)} %modes_hbm.1, f32[256,256]{1,0:T(8,128)} %constant.6.clone.rows_hbm, ...), custom_call_target="tpu_custom_call" | custom-call | tf_op jit(solution)/shard_map/pallas_call | solution.py:268
  21.5 2.4 %shard_map.83 = f32[64,4,512]{2,1,0:T(4,128)} custom-call(bf16[4,2,2,64,256]{4,3,2,1,0:T(8,128)(2,1)} %shard_map.82.parts_ref, bf16[256,256]{1,0:T(8,128)(2,1)} %constant.8.clone.flip_ref), custom_call_target="tpu_custom_call" | custom-call | tf_op jit(solution)/shard_map/pallas_call | solution.py:322
